TPU v7x, 32 devices: a whole 2x2x4 slice. The times are simulated.
32 devices in a mesh: grp: 1, row: 32 (over z, y, x, core).
Axes of the slice: x: 2, y: 2, z: 4, core: 2. Of those that a mesh axis runs over, the one named last changes fastest.
Arguments:
- homolog_matrix: bfloat16 [64, 128, 256], P(('grp', 'row')), may hold values from -6 to 6
- alignment_mask: int32 [64, 128], P(('grp', 'row')), may hold values from 0 to 1, as said below
- pair_state_input: bfloat16 [128, 128, 128], P(('grp', 'row')), may hold values from -3 to 3
- chain_label: int32 [128], P('grp'), may hold values from 0 to 3, never falling along the last dimension, each value on 1 to 64 neighbouring positions
- residue_number_index: int32 [128], P('grp'), may hold values from 1 to 382, as said below
- relative_position_table: float32 [66, 128], replicated, may hold values from -3 to 3
- tensor_factor_coefficients: bfloat16 [256, 64], replicated, may hold values from -0.375 to 0.375
- outer_output_weight: bfloat16 [1024, 128], replicated, may hold values from -3 to 3
- scorer_entry_coefficients: bfloat16 [256, 1024], replicated, may hold values from -0.375 to 0.375
- scorer_final_coefficients: bfloat16 [256, 256], replicated, may hold values from -0.375 to 0.375
- pair_bias_weight: bfloat16 [128, 8], replicated
- triangle_input_weight: bfloat16 [128, 512], replicated, may hold values from -0.5 to 0.5
- triangle_output_gate: bfloat16 [128, 128], replicated, may hold values from -1.5 to 1.5
- triangle_output_weight: bfloat16 [128, 128], replicated, may hold values from -1.796875 to 1.796875
Outputs:
- homolog_revised: bfloat16 [64, 128, 256], P(('grp', 'row'))
- pair_state_output: bfloat16 [128, 128, 128], P(('grp', 'row'))
Inputs may be any that keep to these rules, and one draw needn't show every extreme that they name: `alignment_mask`: 1 marks a live entry of an MSA row. `chain_label`: chain ids never fall along the residues; a chain holds at most 64 residues. `residue_number_index`: residue numbers strictly increase along the residues.
All inputs are finite; a program needn't handle non-finite values.
Results may differ from a plain program's by a relative error of at most 0.03.
Values may be sent and summed in bfloat16 or wider, within the bound.
A program may use at most 128 MiB of HBM per device.

v0:
```python
import jax
import jax.numpy as jnp
from jax import lax
from jax.sharding import PartitionSpec as P

REL_MAX = 32


def layer_normalize(values):
    centre = jnp.mean(values, axis=-1, keepdims=True)
    shifted = values - centre
    spread = jnp.mean(shifted * shifted, axis=-1, keepdims=True)
    return shifted * lax.rsqrt(spread + 1e-05)


def on_device(
    homolog_matrix,
    alignment_mask,
    pair_state_input,
    chain_label,
    residue_number_index,
    relative_position_table,
    tensor_factor_coefficients,
    outer_output_weight,
    scorer_entry_coefficients,
    scorer_final_coefficients,
    pair_bias_weight,
    triangle_input_weight,
    triangle_output_gate,
    triangle_output_weight,
):
    sequence_local_rows = homolog_matrix.shape[0]
    residue_total = homolog_matrix.shape[1]
    alignment_width = homolog_matrix.shape[2]
    res_local = pair_state_input.shape[0]
    pair_width = pair_state_input.shape[2]
    opm_width = tensor_factor_coefficients.shape[1] // 2
    head_total = pair_bias_weight.shape[1]
    head_channel_width = alignment_width // head_total
    tri_width = triangle_input_weight.shape[1] // 4
    table_rows = relative_position_table.shape[0]
    row_start = lax.axis_index("row") * res_local
    contract = (((0,), (0,)), ((), ()))
    active_entry_mask = alignment_mask.astype(jnp.float32)
    homolog_rescaled = layer_normalize(homolog_matrix.astype(jnp.float32)).astype(jnp.bfloat16)
    homolog_lines_merged = homolog_rescaled.reshape(
        sequence_local_rows * residue_total, alignment_width
    )
    projected_rows = jnp.dot(
        homolog_lines_merged, tensor_factor_coefficients, preferred_element_type=jnp.float32
    ).reshape(sequence_local_rows, residue_total, 2 * opm_width)
    left_factor = (
        (projected_rows[..., :opm_width] * active_entry_mask[..., None])
        .astype(jnp.bfloat16)
        .reshape(sequence_local_rows, residue_total * opm_width)
    )
    right_factor = (
        (projected_rows[..., opm_width:] * active_entry_mask[..., None])
        .astype(jnp.bfloat16)
        .reshape(sequence_local_rows, residue_total * opm_width)
    )
    live_weights = active_entry_mask.astype(jnp.bfloat16)
    left_all, right_all, live_all = (
        lax.all_gather(left_factor, "row", axis=0, tiled=True),
        lax.all_gather(right_factor, "row", axis=0, tiled=True),
        lax.all_gather(live_weights, "row", axis=0, tiled=True),
    )
    left_cols = lax.dynamic_slice_in_dim(left_all, row_start * opm_width, res_local * opm_width, 1)
    live_cols = lax.dynamic_slice_in_dim(live_all, row_start, res_local, 1)
    outer_sum = lax.dot_general(left_cols, right_all, contract, preferred_element_type=jnp.float32)
    pair_count = lax.dot_general(live_cols, live_all, contract, preferred_element_type=jnp.float32)
    outer_flat = outer_sum.reshape(res_local, opm_width, residue_total, opm_width).transpose(
        0, 2, 1, 3
    )
    outer_flat = outer_flat.reshape(res_local * residue_total, opm_width * opm_width).astype(
        jnp.bfloat16
    )
    opm_update = jnp.dot(
        outer_flat, outer_output_weight, preferred_element_type=jnp.float32
    ).reshape(res_local, residue_total, pair_width)
    opm_update = opm_update / (0.001 + pair_count[..., None])
    chain_rows = lax.dynamic_slice_in_dim(chain_label, row_start, res_local, 0)
    index_rows = lax.dynamic_slice_in_dim(residue_number_index, row_start, res_local, 0)
    same_chain = chain_rows[:, None] == chain_label[None, :]
    offsets = (
        jnp.clip(index_rows[:, None] - residue_number_index[None, :], -REL_MAX, REL_MAX) + REL_MAX
    )
    bin_index = jnp.where(same_chain, offsets, 2 * REL_MAX + 1)
    one_hot = (
        (bin_index[..., None] == jnp.arange(table_rows, dtype=jnp.int32))
        .astype(jnp.float32)
        .reshape(-1, table_rows)
    )
    position_term = jnp.dot(
        one_hot, relative_position_table, precision=lax.Precision.HIGHEST
    ).reshape(res_local, residue_total, pair_width)
    updated = (pair_state_input.astype(jnp.float32) + position_term + opm_update).astype(
        jnp.bfloat16
    )
    pair_norm = layer_normalize(updated.astype(jnp.float32)).astype(jnp.bfloat16)
    pair_flat = pair_norm.reshape(res_local * residue_total, pair_width)
    head_bias = jnp.dot(pair_flat, pair_bias_weight, preferred_element_type=jnp.float32).astype(
        jnp.bfloat16
    )
    head_bias = head_bias.reshape(res_local, residue_total, head_total).transpose(2, 0, 1)
    full_bias = lax.all_gather(head_bias, "row", axis=1, tiled=True)
    tri_projected = jnp.dot(pair_flat, triangle_input_weight, preferred_element_type=jnp.float32)
    tri_left = (
        jax.nn.sigmoid(tri_projected[:, :tri_width]) * tri_projected[:, tri_width : 2 * tri_width]
    ).astype(jnp.bfloat16)
    tri_right = (
        jax.nn.sigmoid(tri_projected[:, 2 * tri_width : 3 * tri_width])
        * tri_projected[:, 3 * tri_width :]
    ).astype(jnp.bfloat16)
    tri_left = tri_left.reshape(res_local, residue_total, tri_width).transpose(2, 0, 1)
    tri_right = tri_right.reshape(res_local, residue_total, tri_width).transpose(2, 0, 1)
    left_channels, right_channels = (
        lax.all_to_all(tri_left, "row", split_axis=0, concat_axis=1, tiled=True),
        lax.all_to_all(tri_right, "row", split_axis=0, concat_axis=1, tiled=True),
    )
    channel_sum = jnp.einsum(
        "cki,ckj->cij", left_channels, right_channels, preferred_element_type=jnp.float32
    ).astype(jnp.bfloat16)
    row_sum = lax.all_to_all(channel_sum, "row", split_axis=1, concat_axis=0, tiled=True)
    tri_sum = row_sum.transpose(1, 2, 0)
    tri_normed = (
        layer_normalize(tri_sum.astype(jnp.float32))
        .astype(jnp.bfloat16)
        .reshape(res_local * residue_total, tri_width)
    )
    tri_gating = jax.nn.sigmoid(
        jnp.dot(pair_flat, triangle_output_gate, preferred_element_type=jnp.float32)
    )
    pair_state_output = updated.astype(jnp.float32).reshape(
        res_local * residue_total, pair_width
    ) + tri_gating * jnp.dot(tri_normed, triangle_output_weight, preferred_element_type=jnp.float32)
    pair_state_output = pair_state_output.astype(jnp.bfloat16).reshape(
        res_local, residue_total, pair_width
    )
    scorer_mapped_lines = jnp.dot(
        homolog_lines_merged, scorer_entry_coefficients, preferred_element_type=jnp.float32
    )
    asking_vectors = (
        scorer_mapped_lines[:, :alignment_width]
        .astype(jnp.bfloat16)
        .reshape(sequence_local_rows, residue_total, head_total, head_channel_width)
    )
    lookup_lines = (
        scorer_mapped_lines[:, alignment_width : 2 * alignment_width]
        .astype(jnp.bfloat16)
        .reshape(sequence_local_rows, residue_total, head_total, head_channel_width)
    )
    content_lines = (
        scorer_mapped_lines[:, 2 * alignment_width : 3 * alignment_width]
        .astype(jnp.bfloat16)
        .reshape(sequence_local_rows, residue_total, head_total, head_channel_width)
    )
    sigmoid_factor = (
        scorer_mapped_lines[:, 3 * alignment_width :]
        .astype(jnp.bfloat16)
        .reshape(sequence_local_rows, residue_total, head_total, head_channel_width)
    )
    mask_term = 1000000000.0 * (active_entry_mask - 1.0)
    score_scale = head_channel_width ** (-0.5)

    def attend(row_inputs):
        query_row, key_row, value_row, gate_row, mask_row = row_inputs
        scores = (
            jnp.einsum("ihd,jhd->hij", query_row, key_row, preferred_element_type=jnp.float32)
            * score_scale
        )
        scores = scores + full_bias.astype(jnp.float32) + mask_row[None, None, :]
        weights = jax.nn.softmax(scores, axis=-1).astype(jnp.bfloat16)
        attended = jnp.einsum(
            "hij,jhd->ihd", weights, value_row, preferred_element_type=jnp.float32
        )
        return (jax.nn.sigmoid(gate_row.astype(jnp.float32)) * attended).astype(jnp.bfloat16)

    sigmoid_scaled_lines = lax.map(
        attend, (asking_vectors, lookup_lines, content_lines, sigmoid_factor, mask_term)
    )
    homolog_revised = homolog_matrix.astype(jnp.float32).reshape(
        sequence_local_rows * residue_total, alignment_width
    ) + jnp.dot(
        sigmoid_scaled_lines.reshape(sequence_local_rows * residue_total, alignment_width),
        scorer_final_coefficients,
        preferred_element_type=jnp.float32,
    )
    homolog_revised = homolog_revised.astype(jnp.bfloat16).reshape(
        sequence_local_rows, residue_total, alignment_width
    )
    return (homolog_revised, pair_state_output)


def solution(mesh):
    return jax.shard_map(
        on_device,
        mesh=mesh,
        in_specs=(
            P(("grp", "row"), None, None),
            P(("grp", "row"), None),
            P(("grp", "row"), None, None),
            P("grp"),
            P("grp"),
            P(),
            P(),
            P(),
            P(),
            P(),
            P(),
            P(),
            P(),
            P(),
        ),
        out_specs=(P(("grp", "row"), None, None), P(("grp", "row"), None, None)),
        check_vma=False,
    )
```

profile of v0, /device:TPU:0, one launch (start us, length us, event | category | flops | bytes accessed | tf_op | source)
XLA Modules:
  0.0 210.1 jit_solution(4078920670390650498)
XLA Ops:
  0.6 0.0 copy-start
  0.6 1.1 convert_reduce_fusion
  1.7 1.1 multiply_reduce_fusion.2
  2.8 1.0 multiply_convert_fusion.2
  3.9 0.7 convert_bitcast_fusion
  4.6 0.9 fusion.51
  5.5 0.1 copy.73
  5.7 0.1 reshape.208
  5.8 44.6 %all-gather = bf16[32,2,4096]{2,1,0:T(2,128)(2,1)S(1)} all-gather(bf16[1,2,4096]{2,1,0:T(2,128)(2,1)S(1)} %reshape.208), channel_id=1, replica_groups=mesh['grp'=1,'row'=32] {'row'}, dimensions={0}, use_global_device_ids=true | all-gather | bytes 540672 | tf_op jit(solution)/shard_map/all_gather | solution.py:64
  50.4 0.2 reshape.209
  50.6 0.1 copy.74
  50.8 0.1 reshape.210
  50.9 38.1 %all-gather.1 = bf16[32,2,4096]{2,1,0:T(2,128)(2,1)S(1)} all-gather(bf16[1,2,4096]{2,1,0:T(2,128)(2,1)S(1)} %reshape.210), channel_id=1, replica_groups=mesh['grp'=1,'row'=32] {'row'}, dimensions={0}, use_global_device_ids=true | all-gather | bytes 540672 | tf_op jit(solution)/shard_map/all_gather | solution.py:65
  88.9 0.2 reshape.211
  89.2 0.5 convolution_convert_fusion
  89.6 0.0 copy-start.11
  89.7 4.5 %convert_element_type.106 = bf16[4,32,128,32]{3,2,1,0:T(8,128)(2,1)} reshape(bf16[128,4096]{1,0:T(8,128)(2,1)S(1)} %convolution_convert_fusion) | data formatting | bytes 2097152 | tf_op jit(solution)/shard_map/convert_element_type | solution.py:75
  94.1 3.6 %copy.75 = bf16[4,128,32,32]{1,3,2,0:T(8,128)(2,1)S(1)} copy(bf16[4,128,32,32]{3,1,2,0:T(8,128)(2,1)} %bitcast.135) | data formatting | bytes 2097152 | tf_op jit(solution)/shard_map/convert_element_type | solution.py:75
  97.7 37.9 %all-gather.2 = bf16[32,2,128]{2,1,0:T(2,128)(2,1)S(1)} all-gather(bf16[1,2,128]{2,1,0:T(2,128)(2,1)S(1)} %get-tuple-element.101), channel_id=1, replica_groups=mesh['grp'=1,'row'=32] {'row'}, dimensions={0}, use_global_device_ids=true | all-gather | bytes 16896 | tf_op jit(solution)/shard_map/all_gather | solution.py:66
  135.6 0.2 convolution_add_fusion.2
  135.8 0.1 dynamic_slice.29
  135.9 0.1 dynamic_slice.30
  136.0 0.1 add_select_fusion
  136.1 0.5 convolution_divide_fusion
  136.6 0.5 fusion.63
  137.1 0.2 multiply_reduce_fusion.1
  137.3 0.2 multiply_convert_fusion.1
  137.6 0.3 fusion.64
  137.8 0.0 copy-start.7
  137.9 0.1 fusion.36
  138.0 0.8 copy.83
  138.8 2.6 %all-to-all-start = ((bf16[128,4,128]{2,1,0:T(4,128)(2,1)}), bf16[128,4,128]{2,1,0:T(4,128)(2,1)S(1)}, u32[]{:S(2)}, u32[]{:S(2)}) async-start(bf16[128,4,128]{2,1,0:T(4,128)(2,1)} %bitcast.22), calls=%async_computation | async-start | bytes 262144 | tf_op jit(solution)/shard_map/all_to_all | solution.py:118
  141.4 0.1 fusion.35
  141.5 0.3 convolution_convert_fusion.1
  141.9 42.5 %all_gather.15 = bf16[8,128,128]{2,0,1:T(8,128)(2,1)S(1)} all-gather(bf16[8,4,128]{2,0,1:T(8,128)(2,1)S(1)} %fusion.35), channel_id=1, replica_groups=mesh['grp'=1,'row'=32] {'row'}, dimensions={1}, use_global_device_ids=true | all-gather | bytes 270336 | tf_op jit(solution)/shard_map/all_gather | solution.py:106
  184.4 0.8 copy.86
  185.2 0.2 copy.81
  185.4 0.1 copy.69
  185.6 0.1 copy.70
  185.8 0.1 copy.71
  185.9 0.1 copy.72
  186.1 2.6 %all-to-all-start.1 = ((bf16[128,4,128]{2,1,0:T(4,128)(2,1)}), bf16[128,4,128]{2,1,0:T(4,128)(2,1)S(1)}, u32[]{:S(2)}, u32[]{:S(2)}) async-start(bf16[128,4,128]{2,1,0:T(4,128)(2,1)} %bitcast.27), calls=%async_computation.1 | async-start | bytes 262144 | tf_op jit(solution)/shard_map/all_to_all | solution.py:119
  188.8 0.0 copy-start.1
  188.8 0.0 copy-start.4
  188.8 2.0 while.10
  188.8 0.3 fusion.101
  189.1 0.4 fusion.100
  189.5 0.3 fusion.102
  189.8 0.3 fusion.101
  190.1 0.4 fusion.100
  190.5 0.3 fusion.102
  190.8 0.0 copy-start.6
  190.8 0.1 copy.85
  190.9 6.1 %all-to-all-done.1 = bf16[128,4,128]{2,1,0:T(4,128)(2,1)S(1)} async-done(((bf16[128,4,128]{2,1,0:T(4,128)(2,1)}), bf16[128,4,128]{2,1,0:T(4,128)(2,1)S(1)}, u32[]{:S(2)}, u32[]{:S(2)}) %all-to-all-start.1) | async-done | bytes 131104 | tf_op jit(solution)/shard_map/all_to_all | solution.py:119
  197.0 0.1 copy.88
  197.1 0.2 convolution_convert_fusion.2
  197.3 0.8 copy.90
  198.1 2.6 %all-to-all-start.2 = ((bf16[4,128,128]{2,0,1:T(4,128)(2,1)}), bf16[4,128,128]{2,0,1:T(4,128)(2,1)S(1)}, u32[]{:S(2)}, u32[]{:S(2)}) async-start(bf16[4,128,128]{2,0,1:T(4,128)(2,1)} %copy.90), calls=%async_computation.2 | async-start | bytes 262144 | tf_op jit(solution)/shard_map/all_to_all | solution.py:124
  200.7 0.2 fusion.29
  200.9 0.1 copy.82
  201.1 0.9 fusion.33
  202.0 6.9 %all-to-all-done.2 = bf16[4,128,128]{2,0,1:T(4,128)(2,1)S(1)} async-done(((bf16[4,128,128]{2,0,1:T(4,128)(2,1)}), bf16[4,128,128]{2,0,1:T(4,128)(2,1)S(1)}, u32[]{:S(2)}, u32[]{:S(2)}) %all-to-all-start.2) | async-done | bytes 131104 | tf_op jit(solution)/shard_map/all_to_all | solution.py:124
  209.1 0.1 copy.92
  209.2 0.8 fusion.34
  (47 shorter events, 0.6 us)
Async XLA Ops:
  0.6 140.9 %copy-start = (bf16[256,1024]{1,0:T(8,128)(2,1)S(1)}, bf16[256,1024]{1,0:T(8,128)(2,1)}, u32[]{:S(2)}) copy-start(bf16[256,1024]{1,0:T(8,128)(2,1)} %param.24) | copy-start | bytes 1572868
  89.6 46.2 %copy-start.10 = (s32[128]{0:T(128)S(1)}, s32[128]{0:T(128)}, u32[]{:S(2)}) copy-start(s32[128]{0:T(128)} %param.19) | copy-start | bytes 1540
  89.6 46.3 %copy-start.9 = (s32[128]{0:T(128)S(1)}, s32[128]{0:T(128)}, u32[]{:S(2)}) copy-start(s32[128]{0:T(128)} %param.20) | copy-start | bytes 1540
  89.6 46.4 %copy-start.11 = (bf16[1024,128]{1,0:T(8,128)(2,1)S(1)}, bf16[1024,128]{1,0:T(8,128)(2,1)}, u32[]{:S(2)}) copy-start(bf16[1024,128]{1,0:T(8,128)(2,1)} %param.23) | copy-start | bytes 786436
  94.1 42.5 %copy-start.3 = (bf16[4,128,128]{2,1,0:T(8,128)(2,1)S(1)}, bf16[4,128,128]{2,1,0:T(8,128)(2,1)}, u32[]{:S(2)}) copy-start(bf16[4,128,128]{2,1,0:T(8,128)(2,1)} %param.18) | copy-start | bytes 393220
  94.1 42.5 %copy-start.5 = (f32[66,128]{1,0:T(8,128)S(1)}, f32[66,128]{1,0:T(8,128)}, u32[]{:S(2)}) copy-start(f32[66,128]{1,0:T(8,128)} %param.21) | copy-start | bytes 101380
  94.1 43.4 %copy-start.2 = (bf16[128,512]{1,0:T(8,128)(2,1)S(1)}, bf16[128,512]{1,0:T(8,128)(2,1)}, u32[]{:S(2)}) copy-start(bf16[128,512]{1,0:T(8,128)(2,1)} %param.27) | copy-start | bytes 393220
  97.7 43.7 %copy-start.8 = (bf16[128,8]{0,1:T(8,128)(2,1)S(1)}, bf16[128,8]{0,1:T(8,128)(2,1)}, u32[]{:S(2)}) copy-start(bf16[128,8]{0,1:T(8,128)(2,1)} %param.26) | copy-start | bytes 6148
  137.8 48.3 %copy-start.7 = (s32[2,128]{1,0:T(2,128)S(1)}, s32[2,128]{1,0:T(2,128)}, u32[]{:S(2)}) copy-start(s32[2,128]{1,0:T(2,128)} %param.17) | copy-start | bytes 3076
  138.8 47.3 %all-to-all-start = ((bf16[128,4,128]{2,1,0:T(4,128)(2,1)}), bf16[128,4,128]{2,1,0:T(4,128)(2,1)S(1)}, u32[]{:S(2)}, u32[]{:S(2)}) async-start(bf16[128,4,128]{2,1,0:T(4,128)(2,1)} %bitcast.22), calls=%async_computation | async-start | bytes 262144 | tf_op jit(solution)/shard_map/all_to_all | solution.py:118
  186.1 10.8 %all-to-all-start.1 = ((bf16[128,4,128]{2,1,0:T(4,128)(2,1)}), bf16[128,4,128]{2,1,0:T(4,128)(2,1)S(1)}, u32[]{:S(2)}, u32[]{:S(2)}) async-start(bf16[128,4,128]{2,1,0:T(4,128)(2,1)} %bitcast.27), calls=%async_computation.1 | async-start | bytes 262144 | tf_op jit(solution)/shard_map/all_to_all | solution.py:119
  188.7 11.9 %copy-start.12 = (bf16[128,128]{1,0:T(8,128)(2,1)S(1)}, bf16[128,128]{1,0:T(8,128)(2,1)}, u32[]{:S(2)}) copy-start(bf16[128,128]{1,0:T(8,128)(2,1)} %param.28) | copy-start | bytes 98308
  188.8 12.3 %copy-start.1 = (bf16[2,128,256]{2,1,0:T(8,128)(2,1)S(1)}, bf16[2,128,256]{2,1,0:T(8,128)(2,1)}, u32[]{:S(2)}) copy-start(bf16[2,128,256]{2,1,0:T(8,128)(2,1)} %param.16) | copy-start | bytes 393220
  188.8 12.3 %copy-start.4 = (bf16[256,256]{1,0:T(8,128)(2,1)S(1)}, bf16[256,256]{1,0:T(8,128)(2,1)}, u32[]{:S(2)}) copy-start(bf16[256,256]{1,0:T(8,128)(2,1)} %param.25) | copy-start | bytes 393220
  190.8 18.5 %copy-start.6 = (bf16[128,128]{1,0:T(8,128)(2,1)S(1)}, bf16[128,128]{1,0:T(8,128)(2,1)}, u32[]{:S(2)}) copy-start(bf16[128,128]{1,0:T(8,128)(2,1)} %param.29) | copy-start | bytes 98308
  198.1 10.8 %all-to-all-start.2 = ((bf16[4,128,128]{2,0,1:T(4,128)(2,1)}), bf16[4,128,128]{2,0,1:T(4,128)(2,1)S(1)}, u32[]{:S(2)}, u32[]{:S(2)}) async-start(bf16[4,128,128]{2,0,1:T(4,128)(2,1)} %copy.90), calls=%async_computation.2 | async-start | bytes 262144 | tf_op jit(solution)/shard_map/all_to_all | solution.py:124
where the time goes:
time: 211 us; the launch traced here: 210 us
  blocking collectives  163 us (77%)
  local copies, waits for them, and re-layouts  13 us (6%)
  waiting for transfers between devices  13 us (6%)
  starting transfers between devices  7.74 us (4%)
  matrix products  7.36 us (3%)
  other arithmetic  4.76 us (2%)
    all_gather x1, blocking collectives, on_device(): lax.all_gather(left_factor, 'row', axis=0, tiled=True)  44.6 us
    all_gather x1, blocking collectives, on_device(): full_bias = lax.all_gather(head_bias, 'row', axis=1, tiled=True)  42.5 us
    all_gather x1, blocking collectives, on_device(): lax.all_gather(right_factor, 'row', axis=0, tiled=True)  38.1 us
    all_gather x1, blocking collectives, on_device(): lax.all_gather(live_weights, 'row', axis=0, tiled=True)  37.9 us
    convert_element_type x2, local copies, waits for them, and re-layouts, on_device(): outer_flat.reshape(res_local * residue_total, opm_width * opm_width)  8.06 us
    all_to_all x1, waiting for transfers between devices, on_device(): lax.all_to_all(channel_sum, 'row', split_axis=1, concat_axis=0, tiled=True)  6.94 us
    all_to_all x1, waiting for transfers between devices, on_device(): lax.all_to_all(tri_right, 'row', split_axis=0, concat_axis=1, tiled=True)  6.06 us
  transfers between devices with their start and end apart: 3, of which 2 were waited for; matrix products, arithmetic and copies ran while one was open for 3% of the time, Pallas kernels for 0%

commit v1 on v0

--- a/solution.py
+++ b/solution.py
@@ -116,7 +116,12 @@
     tri_right = tri_right.reshape(res_local, residue_total, tri_width).transpose(2, 0, 1)
     left_channels, right_channels = (
         lax.all_to_all(tri_left, "row", split_axis=0, concat_axis=1, tiled=True),
-        lax.all_to_all(tri_right, "row", split_axis=0, concat_axis=1, tiled=True),
+        jnp.concatenate(
+            lax.all_to_all(
+                jnp.stack(jnp.split(tri_right, lax.axis_size("row"), axis=0)), "row", 0, 0
+            ),
+            axis=1,
+        ),
     )
     channel_sum = jnp.einsum(
         "cki,ckj->cij", left_channels, right_channels, preferred_element_type=jnp.float32

time: 211 us -> 262 us (1.24)
  local copies, waits for them, and re-layouts: 13 us -> 63 us
    split x0 -> x34, local copies, waits for them, and re-layouts: none -> 25.2 us  [on_device(): jnp.split(tri_right, lax.axis_size('row'), axis=0)]
    unnamed x30 -> x59, local copies, waits for them, and re-layouts: 0.72 us -> 25.9 us
    all_to_all x1, waiting for transfers between devices: 0.01 us -> 6.15 us  [on_device(): lax.all_to_all(tri_left, 'row', split_axis=0, concat_axis=1, tiled=True)]
    all_to_all x1, waiting for transfers between devices: 6.06 us -> 0.01 us  [on_device(): lax.all_to_all(jnp.stack(jnp.split(tri_right, lax.axis_size('row'), axis=...]
  transfers between devices with their start and end apart: 3 -> 3, of which waited for: 2 -> 2; matrix products, arithmetic and copies ran while one was open for 3% -> 2% of each run, Pallas kernels for 0% -> 0%
where the time goes in v1:
time: 262 us; the launch traced here: 261 us
  blocking collectives  163 us (62%)
  local copies, waits for them, and re-layouts  63 us (24%)
  waiting for transfers between devices  13.1 us (5%)
  matrix products  8.03 us (3%)
  starting transfers between devices  7.73 us (3%)
  other arithmetic  4.78 us (2%)
    all_gather x1, blocking collectives, on_device(): lax.all_gather(left_factor, 'row', axis=0, tiled=True)  44.6 us
    all_gather x1, blocking collectives, on_device(): full_bias = lax.all_gather(head_bias, 'row', axis=1, tiled=True)  42.5 us
    all_gather x1, blocking collectives, on_device(): lax.all_gather(right_factor, 'row', axis=0, tiled=True)  38.1 us
    all_gather x1, blocking collectives, on_device(): lax.all_gather(live_weights, 'row', axis=0, tiled=True)  37.9 us
    unnamed x59, local copies, waits for them, and re-layouts  25.9 us
    split x34, local copies, waits for them, and re-layouts, on_device(): jnp.split(tri_right, lax.axis_size('row'), axis=0)  25.2 us
    convert_element_type x2, local copies, waits for them, and re-layouts, on_device(): outer_flat.reshape(res_local * residue_total, opm_width * opm_width)  8.06 us
    all_to_all x1, waiting for transfers between devices, on_device(): lax.all_to_all(channel_sum, 'row', split_axis=1, concat_axis=0, tiled=True)  6.94 us
  transfers between devices with their start and end apart: 3, of which 2 were waited for; matrix products, arithmetic and copies ran while one was open for 2% of the time, Pallas kernels for 0%

profile of v1, /device:TPU:0, one launch (start us, length us, event | category | flops | bytes accessed | tf_op | source)
XLA Modules:
  0.0 260.9 jit_solution(15427917490330917848)
XLA Ops:
  0.6 1.1 convert_reduce_fusion
  1.7 1.1 multiply_reduce_fusion.2
  2.8 1.0 multiply_convert_fusion.2
  3.9 0.7 convert_bitcast_fusion.1
  4.6 0.9 fusion.51
  5.8 44.6 %all-gather = bf16[32,2,4096]{2,1,0:T(2,128)(2,1)S(1)} all-gather(bf16[1,2,4096]{2,1,0:T(2,128)(2,1)S(1)} %reshape.216), channel_id=1, replica_groups=mesh['grp'=1,'row'=32] {'row'}, dimensions={0}, use_global_device_ids=true | all-gather | bytes 540672 | tf_op jit(solution)/shard_map/all_gather | solution.py:64
  50.9 38.1 %all-gather.1 = bf16[32,2,4096]{2,1,0:T(2,128)(2,1)S(1)} all-gather(bf16[1,2,4096]{2,1,0:T(2,128)(2,1)S(1)} %reshape.218), channel_id=1, replica_groups=mesh['grp'=1,'row'=32] {'row'}, dimensions={0}, use_global_device_ids=true | all-gather | bytes 540672 | tf_op jit(solution)/shard_map/all_gather | solution.py:65
  89.7 4.5 %convert_element_type.106 = bf16[4,32,128,32]{3,2,1,0:T(8,128)(2,1)} reshape(bf16[128,4096]{1,0:T(8,128)(2,1)S(1)} %convolution_convert_fusion) | data formatting | bytes 2097152 | tf_op jit(solution)/shard_map/convert_element_type | solution.py:75
  94.1 3.6 %copy.1729 = bf16[4,128,32,32]{1,3,2,0:T(8,128)(2,1)S(1)} copy(bf16[4,128,32,32]{3,1,2,0:T(8,128)(2,1)} %bitcast.201) | data formatting | bytes 2097152 | tf_op jit(solution)/shard_map/convert_element_type | solution.py:75
  97.7 37.9 %all-gather.2 = bf16[32,2,128]{2,1,0:T(2,128)(2,1)S(1)} all-gather(bf16[1,2,128]{2,1,0:T(2,128)(2,1)S(1)} %get-tuple-element.365), channel_id=1, replica_groups=mesh['grp'=1,'row'=32] {'row'}, dimensions={0}, use_global_device_ids=true | all-gather | bytes 16896 | tf_op jit(solution)/shard_map/all_gather | solution.py:66
  138.0 1.7 fusion.64
  139.7 1.4 fusion.63
  141.1 1.0 copy.1740
  142.1 0.6 constant_dynamic-update-slice_fusion.31
  142.7 1.6 copy.1741
  144.3 1.6 copy.1742
  145.9 1.6 copy.1743
  147.5 1.6 copy.1744
  149.1 1.6 copy.1745
  150.7 1.6 copy.1746
  152.3 1.6 copy.1747
  153.8 1.6 copy.1748
  155.4 1.6 copy.1749
  157.0 1.6 copy.1750
  158.6 1.0 copy.1751
  159.6 1.0 copy.1752
  160.6 1.0 copy.1753
  163.8 1.3 constant_dynamic-update-slice_fusion.30
  165.1 1.3 constant_dynamic-update-slice_fusion.29
  166.3 1.3 constant_dynamic-update-slice_fusion.28
  167.6 1.3 constant_dynamic-update-slice_fusion.27
  168.9 1.3 constant_dynamic-update-slice_fusion.26
  170.1 1.3 constant_dynamic-update-slice_fusion.25
  171.4 1.3 constant_dynamic-update-slice_fusion.24
  172.7 1.3 constant_dynamic-update-slice_fusion.23
  173.9 1.3 constant_dynamic-update-slice_fusion.22
  175.2 1.3 constant_dynamic-update-slice_fusion.21
  176.5 0.6 constant_dynamic-update-slice_fusion.20
  177.1 0.6 constant_dynamic-update-slice_fusion.19
  177.7 0.6 constant_dynamic-update-slice_fusion.18
  178.3 0.6 constant_dynamic-update-slice_fusion.17
  178.9 0.6 constant_dynamic-update-slice_fusion.16
  180.0 0.6 constant_dynamic-update-slice_fusion.14
  180.6 0.6 constant_dynamic-update-slice_fusion.13
  181.2 0.6 constant_dynamic-update-slice_fusion.12
  182.4 0.6 constant_dynamic-update-slice_fusion.10
  183.6 0.6 constant_dynamic-update-slice_fusion.8
  184.8 0.6 constant_dynamic-update-slice_fusion.6
  185.4 0.6 constant_dynamic-update-slice_fusion.5
  186.0 0.6 constant_dynamic-update-slice_fusion.4
  186.6 0.6 constant_dynamic-update-slice_fusion.3
  187.8 0.6 constant_dynamic-update-slice_fusion.1
  188.9 2.6 all-to-all-start.1
  191.5 0.8 fusion.35
  192.7 42.5 %all_gather.15 = bf16[8,128,128]{2,0,1:T(8,128)(2,1)S(1)} all-gather(bf16[8,4,128]{2,0,1:T(8,128)(2,1)S(1)} %fusion.35), channel_id=1, replica_groups=mesh['grp'=1,'row'=32] {'row'}, dimensions={1}, use_global_device_ids=true | all-gather | bytes 270336 | tf_op jit(solution)/shard_map/all_gather | solution.py:106
  235.2 0.8 copy.1737
  236.9 2.6 all-to-all-start
  239.6 2.0 while.10
  241.6 6.2 %all-to-all-done = bf16[128,4,128]{2,1,0:T(4,128)(2,1)S(1)} async-done(((bf16[128,4,128]{2,1,0:T(4,128)(2,1)}), bf16[128,4,128]{2,1,0:T(4,128)(2,1)S(1)}, u32[]{:S(2)}, u32[]{:S(2)}) %all-to-all-start) | async-done | bytes 131104 | tf_op jit(solution)/shard_map/all_to_all | solution.py:118
  248.1 0.8 copy.1774
  248.9 2.6 all-to-all-start.2
  251.9 0.9 fusion.33
  252.8 6.9 %all-to-all-done.2 = bf16[4,128,128]{2,0,1:T(4,128)(2,1)S(1)} async-done(((bf16[4,128,128]{2,0,1:T(4,128)(2,1)}), bf16[4,128,128]{2,0,1:T(4,128)(2,1)S(1)}, u32[]{:S(2)}, u32[]{:S(2)}) %all-to-all-start.2) | async-done | bytes 131104 | tf_op jit(solution)/shard_map/all_to_all | solution.py:129
  260.1 0.8 fusion.34
  (110 shorter events, 13.7 us)
Async XLA Ops:
  0.6 191.7 %copy-start = (bf16[256,1024]{1,0:T(8,128)(2,1)S(1)}, bf16[256,1024]{1,0:T(8,128)(2,1)}, u32[]{:S(2)}) copy-start(bf16[256,1024]{1,0:T(8,128)(2,1)} %param.24) | copy-start | bytes 1572868
  89.6 46.2 %copy-start.9 = (s32[128]{0:T(128)S(1)}, s32[128]{0:T(128)}, u32[]{:S(2)}) copy-start(s32[128]{0:T(128)} %param.19) | copy-start | bytes 1540
  89.6 46.3 %copy-start.8 = (s32[128]{0:T(128)S(1)}, s32[128]{0:T(128)}, u32[]{:S(2)}) copy-start(s32[128]{0:T(128)} %param.20) | copy-start | bytes 1540
  89.6 46.4 %copy-start.10 = (bf16[1024,128]{1,0:T(8,128)(2,1)S(1)}, bf16[1024,128]{1,0:T(8,128)(2,1)}, u32[]{:S(2)}) copy-start(bf16[1024,128]{1,0:T(8,128)(2,1)} %param.23) | copy-start | bytes 786436
  94.1 42.5 %copy-start.3 = (bf16[4,128,128]{2,1,0:T(8,128)(2,1)S(1)}, bf16[4,128,128]{2,1,0:T(8,128)(2,1)}, u32[]{:S(2)}) copy-start(bf16[4,128,128]{2,1,0:T(8,128)(2,1)} %param.18) | copy-start | bytes 393220
  94.1 42.5 %copy-start.5 = (f32[66,128]{1,0:T(8,128)S(1)}, f32[66,128]{1,0:T(8,128)}, u32[]{:S(2)}) copy-start(f32[66,128]{1,0:T(8,128)} %param.21) | copy-start | bytes 101380
  94.1 43.4 %copy-start.2 = (bf16[128,512]{1,0:T(8,128)(2,1)S(1)}, bf16[128,512]{1,0:T(8,128)(2,1)}, u32[]{:S(2)}) copy-start(bf16[128,512]{1,0:T(8,128)(2,1)} %param.27) | copy-start | bytes 393220
  162.7 74.2 %copy-start.7 = (s32[2,128]{1,0:T(2,128)S(1)}, s32[2,128]{1,0:T(2,128)}, u32[]{:S(2)}) copy-start(s32[2,128]{1,0:T(2,128)} %param.17) | copy-start | bytes 3076
  188.9 48.0 %all-to-all-start.1 = ((bf16[32,4,4,128]{3,2,1,0:T(4,128)(2,1)}), bf16[32,4,4,128]{3,2,1,0:T(4,128)(2,1)S(1)}, u32[]{:S(2)}, u32[]{:S(2)}) async-start(bf16[32,4,4,128]{3,2,1,0:T(4,128)(2,1)} %constant_dynamic-update-slice_fusion), calls=%async_computation.1 | async-start | bytes 262144 | tf_op jit(solution)/shard_map/all_to_all | solution.py:120
  236.9 10.8 %all-to-all-start = ((bf16[128,4,128]{2,1,0:T(4,128)(2,1)}), bf16[128,4,128]{2,1,0:T(4,128)(2,1)S(1)}, u32[]{:S(2)}, u32[]{:S(2)}) async-start(bf16[128,4,128]{2,1,0:T(4,128)(2,1)} %copy.1737), calls=%async_computation | async-start | bytes 262144 | tf_op jit(solution)/shard_map/all_to_all | solution.py:118
  239.5 11.9 %copy-start.11 = (bf16[128,128]{1,0:T(8,128)(2,1)S(1)}, bf16[128,128]{1,0:T(8,128)(2,1)}, u32[]{:S(2)}) copy-start(bf16[128,128]{1,0:T(8,128)(2,1)} %param.28) | copy-start | bytes 98308
  239.6 12.3 %copy-start.1 = (bf16[2,128,256]{2,1,0:T(8,128)(2,1)S(1)}, bf16[2,128,256]{2,1,0:T(8,128)(2,1)}, u32[]{:S(2)}) copy-start(bf16[2,128,256]{2,1,0:T(8,128)(2,1)} %param.16) | copy-start | bytes 393220
  239.6 12.3 %copy-start.4 = (bf16[256,256]{1,0:T(8,128)(2,1)S(1)}, bf16[256,256]{1,0:T(8,128)(2,1)}, u32[]{:S(2)}) copy-start(bf16[256,256]{1,0:T(8,128)(2,1)} %param.25) | copy-start | bytes 393220
  241.5 18.5 %copy-start.6 = (bf16[128,128]{1,0:T(8,128)(2,1)S(1)}, bf16[128,128]{1,0:T(8,128)(2,1)}, u32[]{:S(2)}) copy-start(bf16[128,128]{1,0:T(8,128)(2,1)} %param.29) | copy-start | bytes 98308
  248.9 10.8 %all-to-all-start.2 = ((bf16[4,128,128]{2,0,1:T(4,128)(2,1)}), bf16[4,128,128]{2,0,1:T(4,128)(2,1)S(1)}, u32[]{:S(2)}, u32[]{:S(2)}) async-start(bf16[4,128,128]{2,0,1:T(4,128)(2,1)} %copy.1774), calls=%async_computation.2 | async-start | bytes 262144 | tf_op jit(solution)/shard_map/all_to_all | solution.py:129
